TPU v7x, 32 devices: a whole 2x2x4 slice. The times are simulated.
32 devices in a mesh: blk: 8 (over z, y), line: 4 (over x, core).
Axes of the slice: x: 2, y: 2, z: 4, core: 2. Of those that a mesh axis runs over, the one named last changes fastest.
Arguments:
- density: float32 [8, 64, 4096], P('blk', 'line'), may hold values from 0.5 to 1.5
- momentum: float32 [8, 3, 64, 4096], P('blk', None, 'line'), may hold values from -0.5 to 0.5
- energy: float32 [8, 64, 4096], P('blk', 'line'), may hold values from 2 to 4
- adjoint: float32 [8, 5, 64, 4096], P('blk', None, 'line'), may hold values from -6 to 6
- partners: int32 [8, 4], P('blk'), may hold values from 0 to 7
- counts: int32 [8], P('blk'), may hold values from 1 to 4, as said below
- orient: int32 [8, 4], P('blk'), may hold values from 0 to 1
Outputs:
- residual: float32 [8, 5, 64, 4096], P('blk', None, 'line')
- correction: float32 [8], P('blk')
Inputs may be any that keep to these rules, and one draw needn't show every extreme that they name: `partners`: slots at or past counts[b] are padding and are not read. `counts`: some block lists 4 partners.
All inputs are finite; a program needn't handle non-finite values.
Results may differ from a plain program's by a relative error of at most 0.0003.
Values sent between devices are 32-bit elements; how exact they have to be, the bound alone decides.
No kernel may reach another device: no remote copies, remote signals or barrier semaphores. Data moves between devices by JAX's collectives and lax.ppermute only.
A program may use at most 64 MiB of HBM per device.

v0:
```python
import jax
import jax.numpy as jnp
from jax import lax
from jax.sharding import PartitionSpec as P

stencil_one = 0.75
stencil_two = -0.15
stencil_three = 1.0 / 60.0
gamma_less = 0.4
viscosity = 0.5
conduction = 1.5
penalty = 4.0


def difference(fields, direction, start_row, extent):
    length = fields.shape[direction]

    def shifted(offset):
        return lax.slice_in_dim(fields, 3 + offset, length - 3 + offset, axis=direction)

    shape_list = [1] * fields.ndim
    shape_list[direction] = length - 6
    global_row = (start_row + 3 + jnp.arange(length - 6, dtype=jnp.int32)).reshape(shape_list)
    central_one = shifted(1) - shifted(-1)
    central_two = shifted(2) - shifted(-2)
    central_three = shifted(3) - shifted(-3)
    interior = stencil_one * central_one + stencil_two * central_two + stencil_three * central_three
    fourth = 2.0 / 3.0 * central_one - 1.0 / 12.0 * central_two
    second = 0.5 * central_one
    forward = shifted(1) - shifted(0)
    backward = shifted(0) - shifted(-1)
    result = jnp.where((global_row == 2) | (global_row == extent - 3), fourth, interior)
    result = jnp.where((global_row == 1) | (global_row == extent - 2), second, result)
    result = jnp.where(global_row == 0, forward, result)
    result = jnp.where(global_row == extent - 1, backward, result)
    return result


def primitives(fields):
    density_raw = fields[:, 0:1]
    density_safe = jnp.where(density_raw == 0.0, 1.0, density_raw)
    velocity = fields[:, 1:4] / density_safe
    kinetic = 0.5 * jnp.sum(fields[:, 1:4] * velocity, axis=1, keepdims=True)
    pressure = gamma_less * (fields[:, 4:5] - kinetic)
    return (velocity, pressure, density_safe)


def direction_residual(fields, direction, start_row, extent, normal_index):
    velocity, pressure, density_safe = primitives(fields)
    primitive = jnp.concatenate([velocity, pressure / density_safe], axis=1)
    gradient = difference(primitive, direction, start_row, extent)
    length = fields.shape[direction]
    middle = lax.slice_in_dim(fields, 3, length - 3, axis=direction)
    mid_velocity = lax.slice_in_dim(velocity, 3, length - 3, axis=direction)
    mid_pressure = lax.slice_in_dim(pressure, 3, length - 3, axis=direction)
    normal_speed = mid_velocity[:, normal_index : normal_index + 1]
    selector = (jnp.arange(3) == normal_index).astype(fields.dtype).reshape(1, 3, 1, 1)
    convective = jnp.concatenate(
        [
            middle[:, normal_index + 1 : normal_index + 2],
            middle[:, 1:4] * normal_speed + mid_pressure * selector,
            (middle[:, 4:5] + mid_pressure) * normal_speed,
        ],
        axis=1,
    )
    viscous = jnp.concatenate(
        [
            jnp.zeros_like(normal_speed),
            viscosity * gradient[:, 0:3],
            viscosity * conduction * gradient[:, 3:4],
        ],
        axis=1,
    )
    return difference(convective - viscous, direction, start_row + 3, extent)


def per_device(density, momentum, energy, adjoint, partners, counts, orient):
    state = jnp.concatenate([density[:, None], momentum, energy[:, None]], axis=1)
    xrows = state.shape[2]
    yextent = state.shape[3]
    line_count = lax.axis_size("line")
    block_count = lax.axis_size("blk")
    xextent = xrows * line_count
    lines = lax.all_to_all(state, "line", split_axis=3, concat_axis=2, tiled=True)
    padded_lines = jnp.pad(lines, ((0, 0), (0, 0), (6, 6), (0, 0)))
    line_part = direction_residual(padded_lines, 2, -6, xextent, 0)
    xpart = lax.all_to_all(line_part, "line", split_axis=2, concat_axis=3, tiled=True)
    padded_y = jnp.pad(state, ((0, 0), (0, 0), (0, 0), (6, 6)))
    ypart = direction_residual(padded_y, 3, -6, yextent, 1)
    result = xpart + ypart
    bottom_row = state[:, :, :, 0]
    gathered = lax.all_gather(bottom_row, "blk", axis=0, tiled=True)
    slots = jnp.arange(partners.shape[1], dtype=jnp.int32)
    listed = partners[0]
    count_here = counts[0]
    weights = jnp.where(slots < count_here, 1.0 / count_here.astype(jnp.float32), jnp.float32(0.0))
    onehot = (listed[:, None] == jnp.arange(block_count, dtype=jnp.int32)[None, :]).astype(
        jnp.float32
    ) * weights[:, None]
    picked = jnp.einsum("kb,bvx->kvx", onehot, gathered, precision=lax.Precision.HIGHEST)
    signs = (
        jnp.ones((partners.shape[1], 5), jnp.float32)
        .at[:, 2]
        .set(1.0 - 2.0 * orient[0].astype(jnp.float32))
    )
    target = jnp.sum(picked * signs[:, :, None], axis=0)[None]
    result = result.at[:, :, :, yextent - 1].add(penalty * (state[:, :, :, yextent - 1] - target))
    total = lax.psum(jnp.sum(adjoint * result), "line")
    correction = (total / (xextent * yextent)).reshape(1)
    return (result, correction)


def solution(mesh):
    return jax.shard_map(
        per_device,
        mesh=mesh,
        in_specs=(
            P("blk", "line", None),
            P("blk", None, "line", None),
            P("blk", "line", None),
            P("blk", None, "line", None),
            P("blk", None),
            P("blk"),
            P("blk", None),
        ),
        out_specs=(P("blk", None, "line", None), P("blk")),
        check_vma=False,
    )
```

profile of v0, /device:TPU:0, one launch (start us, length us, event | category | flops | bytes accessed | tf_op | source)
XLA Modules:
  0.0 212.0 jit_solution(9206048323847633590)
XLA Ops:
  0.6 1.4 pad_maximum_fusion
  2.0 14.9 %copy.63 = f32[1,5,16,4096]{2,0,1,3:T(1,128)} copy(f32[1,5,16,4096]{3,2,1,0:T(8,128)S(1)} %pad_maximum_fusion) | data formatting | bytes 2621440 | tf_op jit(solution)/shard_map/concatenate | solution.py:78
  17.4 34.3 %reduce.12 = f32[4096,5,16]{2,1,0:T(8,128)} reduce(f32[4096,5,1,16]{3,2,1,0:T(1,128)} %bitcast.52, f32[]{:T(128)} %broadcast.383), dimensions={2}, to_apply=%bitcast.41.reduce_sub_computation | reduce | bytes 2621444
  51.7 9.3 %reshape.473 = f32[4,1,81920]{2,1,0:T(1,128)} reshape(f32[4096,5,16]{2,1,0:T(8,128)} %reduce.12) | data formatting | bytes 2621440
  61.0 4.2 %all-to-all-start = ((f32[4,1,81920]{2,1,0:T(1,128)}), f32[4,1,81920]{2,1,0:T(1,128)S(1)}, u32[]{:S(2)}, u32[]{:S(2)}) async-start(f32[4,1,81920]{2,1,0:T(1,128)} %reshape.473), calls=%async_computation | async-start | bytes 2621440 | tf_op jit(solution)/shard_map/all_to_all | solution.py:84
  65.3 0.6 compare_or_fusion.2
  66.7 0.7 compare_reduce_fusion
  68.1 1.3 pad_slice_fusion.35
  69.4 1.7 fusion.35
  71.2 1.0 copy-done.3
  72.2 0.7 slice-done
  73.0 31.8 %all-gather = f32[8,5,16,1]{2,3,1,0:T(1,128)S(1)} all-gather(f32[1,5,16,1]{2,3,1,0:T(1,128)S(1)} %copy.75), channel_id=2, replica_groups=mesh['blk'=8,'line'=4] {'blk'}, dimensions={0}, use_global_device_ids=true | all-gather | bytes 2880 | tf_op jit(solution)/shard_map/all_gather | solution.py:92
  105.4 0.6 fusion.79
  106.5 2.2 %fusion.46 = f32[1,3,16,4102]{3,2,1,0:T(8,128)} fusion(f32[1,5,16,4096]{3,2,1,0:T(8,128)S(1)} %copy-done.1, f32[3]{0:T(128)S(1)} %compare_convert_fusion, f32[16,4102]{1,0:T(8,128)} %get-tuple-element.45, f32[16,4102]{1,0:T(8,128)} %get-tuple-element.43), kind=kLoop, calls=%fused_computation.96 | loop fusion | flops 590688 | bytes 2623372 | tf_op jit(solution)/shard_map/add | solution.py:61
  108.7 1.7 slice_multiply_fusion.3
  110.4 5.5 %reduce.13 = f32[4,81920]{1,0:T(4,128)} reduce(f32[4,1,81920]{2,1,0:T(1,128)S(1)} %all-to-all-done, f32[]{:T(128)} %broadcast.383), dimensions={1}, to_apply=%all_to_all.26.reduce_sub_computation | reduce | bytes 2621444 | tf_op jit(solution)/shard_map/all_to_all | solution.py:84
  115.9 27.3 %reshape.474 = f32[4096,5,1,16]{3,2,1,0:T(1,128)} reshape(f32[4,81920]{1,0:T(4,128)} %reduce.13) | data formatting | bytes 2621440
  143.1 19.8 %copy.64 = f32[1,5,16,4096]{3,2,1,0:T(8,128)} copy(f32[1,5,16,4096]{2,0,1,3:T(1,128)} %bitcast.53) | data formatting | bytes 2621440 | tf_op jit(solution)/shard_map/all_to_all | solution.py:84
  162.9 2.2 %all_to_all.27 = f32[1,5,16,4,1024]{4,3,2,1,0:T(4,128)S(1)} reshape(f32[1,5,16,4096]{3,2,1,0:T(8,128)} %copy.64) | data formatting | bytes 2621440 | tf_op jit(solution)/shard_map/all_to_all | solution.py:84
  165.1 0.7 copy.65
  166.8 1.5 fusion.20
  169.1 1.4 fusion.12
  170.5 2.4 %copy.66 = f32[1,5,64,1024]{3,0,1,2:T(1,128)} copy(f32[1,5,64,1024]{3,2,1,0:T(8,128)S(1)} %fusion.12) | data formatting | bytes 2621440 | tf_op jit(solution)/shard_map/jit(_where)/select_n | solution.py:35
  172.9 4.3 %all-to-all-start.1 = ((f32[1,5,64,1024]{3,0,1,2:T(1,128)}), f32[1,5,64,1024]{3,0,1,2:T(1,128)}, u32[]{:S(2)}, u32[]{:S(2)}) async-start(f32[1,5,64,1024]{3,0,1,2:T(1,128)} %copy.66), calls=%async_computation.1 | async-start | bytes 2621440 | tf_op jit(solution)/shard_map/all_to_all | solution.py:87
  177.2 1.6 maximum_subtract_fusion.1
  178.7 15.7 %all-to-all-done.1 = f32[1,5,64,1024]{3,0,1,2:T(1,128)} async-done(((f32[1,5,64,1024]{3,0,1,2:T(1,128)}), f32[1,5,64,1024]{3,0,1,2:T(1,128)}, u32[]{:S(2)}, u32[]{:S(2)}) %all-to-all-start.1) | async-done | bytes 1310752 | tf_op jit(solution)/shard_map/all_to_all | solution.py:87
  194.5 1.6 copy.67
  196.2 2.1 fusion.6
  198.3 1.0 copy-done.2
  199.4 1.8 scatter-add.4
  201.2 2.7 %multiply_reduce_fusion = f32[]{:T(128)} fusion(f32[1,5,16,4096]{3,2,1,0:T(8,128)} %param.14, f32[1,5,16,4096]{3,2,1,0:T(8,128)} %scatter-add.4), kind=kLoop, calls=%fused_computation.50 | loop fusion | flops 655359 | bytes 2621444 | tf_op jit(solution)/shard_map/reduce_sum | solution.py:108
  203.9 6.4 %psum.7 = f32[]{:T(128)} all-reduce(f32[]{:T(128)} %multiply_reduce_fusion), channel_id=1, replica_groups=mesh['blk'=8,'line'=4] {'line'}, use_global_device_ids=true, to_apply=%region_5.6 | all-reduce | flops 1 | bytes 8 | tf_op jit(solution)/shard_map/psum | solution.py:108
  (48 shorter events, 4.4 us)
Async XLA Ops:
  2.0 66.1 %copy-start = (f32[1,5,16,4096]{3,2,1,0:T(8,128)}, f32[1,5,16,4096]{3,2,1,0:T(8,128)S(1)}, u32[]{:S(2)}) copy-start(f32[1,5,16,4096]{3,2,1,0:T(8,128)S(1)} %pad_maximum_fusion) | copy-start | bytes 3932164
  61.0 49.3 %all-to-all-start = ((f32[4,1,81920]{2,1,0:T(1,128)}), f32[4,1,81920]{2,1,0:T(1,128)S(1)}, u32[]{:S(2)}, u32[]{:S(2)}) async-start(f32[4,1,81920]{2,1,0:T(1,128)} %reshape.473), calls=%async_computation | async-start | bytes 2621440 | tf_op jit(solution)/shard_map/all_to_all | solution.py:84
  71.2 1.0 copy-start.3
  72.1 0.8 slice-start
  72.1 33.3 %copy-start.7 = (s32[1,4]{1,0:T(1,128)S(1)}, s32[1,4]{1,0:T(1,128)}, u32[]{:S(2)}) copy-start(s32[1,4]{1,0:T(1,128)} %param.17) | copy-start | bytes 52
  72.1 34.0 %copy-start.8 = (s32[1,4]{1,0:T(1,128)S(1)}, s32[1,4]{1,0:T(1,128)}, u32[]{:S(2)}) copy-start(s32[1,4]{1,0:T(1,128)} %param.15) | copy-start | bytes 52
  72.1 34.3 %copy-start.1 = (f32[1,5,16,4096]{3,2,1,0:T(8,128)S(1)}, f32[1,5,16,4096]{3,2,1,0:T(8,128)}, u32[]{:S(2)}) copy-start(f32[1,5,16,4096]{3,2,1,0:T(8,128)} %copy-done) | copy-start | bytes 3932164
  166.2 0.7 copy-start.4
  166.2 0.7 copy-start.5
  166.2 0.7 copy-start.6
  172.9 21.6 %all-to-all-start.1 = ((f32[1,5,64,1024]{3,0,1,2:T(1,128)}), f32[1,5,64,1024]{3,0,1,2:T(1,128)}, u32[]{:S(2)}, u32[]{:S(2)}) async-start(f32[1,5,64,1024]{3,0,1,2:T(1,128)} %copy.66), calls=%async_computation.1 | async-start | bytes 2621440 | tf_op jit(solution)/shard_map/all_to_all | solution.py:87
  198.3 1.1 copy-start.2
where the time goes:
time: 213 us; the launch traced here: 212 us
  local copies, waits for them, and re-layouts  84.1 us (39%)
  other arithmetic  61.9 us (29%)
  blocking collectives  38.1 us (18%)
  waiting for transfers between devices  15.7 us (7%)
  starting transfers between devices  8.53 us (4%)
  between operations  3.44 us (2%)
    unnamed x22, local copies, waits for them, and re-layouts  39.8 us
    unnamed x1, other arithmetic  34.3 us
    all_gather x1, blocking collectives, per_device(): gathered = lax.all_gather(bottom_row, 'blk', axis=0, tiled=True)  31.8 us
    all_to_all x3, local copies, waits for them, and re-layouts, per_device(): lax.all_to_all(state, 'line', split_axis=3, concat_axis=2, tiled=True)  22.7 us
    all_to_all x1, waiting for transfers between devices, per_device(): lax.all_to_all(line_part, 'line', split_axis=2, concat_axis=3, tiled=True)  15.7 us
    concatenate x1, local copies, waits for them, and re-layouts, per_device(): jnp.concatenate([density[:, None], momentum, energy[:, None]], axis=1)  14.9 us
    psum x1, blocking collectives, per_device(): total = lax.psum(jnp.sum(adjoint * result), 'line')  6.37 us
    all_to_all x1, other arithmetic, per_device(): lax.all_to_all(state, 'line', split_axis=3, concat_axis=2, tiled=True)  5.48 us
  transfers between devices with their start and end apart: 2, of which 1 were waited for; matrix products, arithmetic and copies ran while one was open for 6% of the time, Pallas kernels for 0%

commit v1 on v0

--- a/solution.py
+++ b/solution.py
@@ -1,3 +1,4 @@
+import functools
 import jax
 import jax.numpy as jnp
 from jax import lax
@@ -10,6 +11,26 @@
 viscosity = 0.5
 conduction = 1.5
 penalty = 4.0
+
+
+def launch_kinds_on(matrix, a_name):
+    n_all = lax.axis_size(a_name)
+    rack = []
+    for i in range(1, n_all):
+        rack.append((i - 1, i))
+    ready = rack + [(n_all - 1, 0)]
+    front = matrix
+    block_list = [front]
+    for _ in range(n_all - 1):
+        front = lax.ppermute(front, a_name, ready)
+        block_list += [front]
+    current_value = jnp.concatenate([*reversed(block_list)], axis=0)
+    found_now = lax.axis_index(a_name)
+    row_out = jnp.roll(current_value, (found_now + 1) * front.shape[0], axis=0)
+    return row_out
+
+
+play_the_frames = functools.partial(launch_kinds_on, a_name="blk")
 
 
 def difference(fields, direction, start_row, extent):
@@ -89,7 +110,7 @@
     ypart = direction_residual(padded_y, 3, -6, yextent, 1)
     result = xpart + ypart
     bottom_row = state[:, :, :, 0]
-    gathered = lax.all_gather(bottom_row, "blk", axis=0, tiled=True)
+    gathered = play_the_frames(bottom_row)
     slots = jnp.arange(partners.shape[1], dtype=jnp.int32)
     listed = partners[0]
     count_here = counts[0]

time: 213 us -> 209 us (0.981)
  blocking collectives: 38.1 us -> 6.27 us
  waiting for transfers between devices: 15.7 us -> 44.1 us
  starting transfers between devices: 8.53 us -> 13.4 us
  other arithmetic: 61.9 us -> 58.6 us
  local copies, waits for them, and re-layouts: 84.1 us -> 81.7 us
    ppermute x0 -> x7, waiting for transfers between devices: none -> 35.3 us  [launch_kinds_on(): front = lax.ppermute(front, a_name, ready)]
    all_gather x1 -> x0, blocking collectives: 31.8 us -> none  [per_device(): gathered = lax.all_gather(bottom_row, 'blk', axis=0, tiled=True)]
    all_to_all x1, waiting for transfers between devices: 15.7 us -> 0.01 us  [per_device(): lax.all_to_all(line_part, 'line', split_axis=2, concat_axis=3, tiled=True)]
    all_to_all x1, waiting for transfers between devices: 0.01 us -> 8.81 us  [per_device(): lax.all_to_all(state, 'line', split_axis=3, concat_axis=2, tiled=True)]
    ppermute x0 -> x7, starting transfers between devices: none -> 4.88 us  [launch_kinds_on(): front = lax.ppermute(front, a_name, ready)]
    unnamed x22 -> x9, local copies, waits for them, and re-layouts: 39.8 us -> 38.2 us
  transfers between devices with their start and end apart: 2 -> 9, of which waited for: 1 -> 7; matrix products, arithmetic and copies ran while one was open for 6% -> 33% of each run, Pallas kernels for 0% -> 0%
where the time goes in v1:
time: 209 us; the launch traced here: 208 us
  local copies, waits for them, and re-layouts  81.7 us (39%)
  other arithmetic  58.6 us (28%)
  waiting for transfers between devices  44.1 us (21%)
  starting transfers between devices  13.4 us (6%)
  blocking collectives  6.27 us (3%)
  between operations  3.41 us (2%)
    unnamed x9, local copies, waits for them, and re-layouts  38.2 us
    ppermute x7, waiting for transfers between devices, launch_kinds_on(): front = lax.ppermute(front, a_name, ready)  35.3 us
    unnamed x1, other arithmetic  34.3 us
    all_to_all x3, local copies, waits for them, and re-layouts, per_device(): lax.all_to_all(state, 'line', split_axis=3, concat_axis=2, tiled=True)  22.7 us
    concatenate x1, local copies, waits for them, and re-layouts, per_device(): jnp.concatenate([density[:, None], momentum, energy[:, None]], axis=1)  14.7 us
    all_to_all x1, waiting for transfers between devices, per_device(): lax.all_to_all(state, 'line', split_axis=3, concat_axis=2, tiled=True)  8.81 us
    psum x1, blocking collectives, per_device(): total = lax.psum(jnp.sum(adjoint * result), 'line')  6.27 us
    all_to_all x1, other arithmetic, per_device(): lax.all_to_all(state, 'line', split_axis=3, concat_axis=2, tiled=True)  5.48 us
  transfers between devices with their start and end apart: 9, of which 7 were waited for; matrix products, arithmetic and copies ran while one was open for 33% of the time, Pallas kernels for 0%

profile of v1, /device:TPU:0, one launch (start us, length us, event | category | flops | bytes accessed | tf_op | source)
XLA Modules:
  0.0 207.8 jit_solution(11850374157598177473)
XLA Ops:
  0.6 1.4 pad_maximum_fusion
  2.0 14.7 %copy.25 = f32[1,5,16,4096]{2,0,1,3:T(1,128)} copy(f32[1,5,16,4096]{3,2,1,0:T(8,128)S(1)} %pad_maximum_fusion) | data formatting | bytes 2621440 | tf_op jit(solution)/shard_map/concatenate | solution.py:99
  17.2 34.3 %reduce.14 = f32[4096,5,16]{2,1,0:T(8,128)} reduce(f32[4096,5,1,16]{3,2,1,0:T(1,128)} %bitcast.49, f32[]{:T(128)} %broadcast.385), dimensions={2}, to_apply=%bitcast.38.reduce_sub_computation | reduce | bytes 2621444
  51.5 9.3 %reshape.473 = f32[4,1,81920]{2,1,0:T(1,128)} reshape(f32[4096,5,16]{2,1,0:T(8,128)} %reduce.14) | data formatting | bytes 2621440
  60.8 4.2 %all-to-all-start = ((f32[4,1,81920]{2,1,0:T(1,128)}), f32[4,1,81920]{2,1,0:T(1,128)S(1)}, u32[]{:S(2)}, u32[]{:S(2)}) async-start(f32[4,1,81920]{2,1,0:T(1,128)} %reshape.473), calls=%async_computation | async-start | bytes 2621440 | tf_op jit(solution)/shard_map/all_to_all | solution.py:105
  65.1 2.5 %collective-permute-start = (f32[1,5,16]{2,0,1:T(1,128)S(1)}, f32[1,5,16]{2,0,1:T(1,128)S(1)}, u32[]{:S(2)}, u32[]{:S(2)}) collective-permute-start(f32[1,5,16]{2,0,1:T(1,128)S(1)} %squeeze.9), channel_id=1, source_target_pairs={{0,4},{4,8},{8,12},{12,16},{16,20},{20,24},{24,28},{28,0},{1,5},{5... | collective-permute-start | bytes 968 | tf_op jit(solution)/shard_map/ppermute | solution.py:25
  68.6 1.1 pad_slice_fusion.35
  69.8 1.7 fusion.35
  71.6 1.2 fusion.46
  73.5 8.8 %all-to-all-done = f32[4,1,81920]{2,1,0:T(1,128)S(1)} async-done(((f32[4,1,81920]{2,1,0:T(1,128)}), f32[4,1,81920]{2,1,0:T(1,128)S(1)}, u32[]{:S(2)}, u32[]{:S(2)}) %all-to-all-start) | async-done | bytes 1310752 | tf_op jit(solution)/shard_map/all_to_all | solution.py:105
  82.3 5.5 %reduce.15 = f32[4,81920]{1,0:T(4,128)} reduce(f32[4,1,81920]{2,1,0:T(1,128)S(1)} %all-to-all-done, f32[]{:T(128)} %broadcast.385), dimensions={1}, to_apply=%all_to_all.26.reduce_sub_computation | reduce | bytes 2621444 | tf_op jit(solution)/shard_map/all_to_all | solution.py:105
  87.8 27.3 %reshape.474 = f32[4096,5,1,16]{3,2,1,0:T(1,128)} reshape(f32[4,81920]{1,0:T(4,128)} %reduce.15) | data formatting | bytes 2621440
  115.1 19.8 %copy.26 = f32[1,5,16,4096]{3,2,1,0:T(8,128)} copy(f32[1,5,16,4096]{2,0,1,3:T(1,128)} %bitcast.50) | data formatting | bytes 2621440 | tf_op jit(solution)/shard_map/all_to_all | solution.py:105
  134.9 2.2 %all_to_all.27 = f32[1,5,16,4,1024]{4,3,2,1,0:T(4,128)S(1)} reshape(f32[1,5,16,4096]{3,2,1,0:T(8,128)} %copy.26) | data formatting | bytes 2621440 | tf_op jit(solution)/shard_map/all_to_all | solution.py:105
  138.2 1.5 fusion.20
  140.5 1.4 fusion.12
  141.9 2.4 %copy.28 = f32[1,5,64,1024]{3,0,1,2:T(1,128)} copy(f32[1,5,64,1024]{3,2,1,0:T(8,128)S(1)} %fusion.12) | data formatting | bytes 2621440 | tf_op jit(solution)/shard_map/jit(_where)/select_n | solution.py:56
  144.3 4.3 %all-to-all-start.1 = ((f32[1,5,64,1024]{3,0,1,2:T(1,128)}), f32[1,5,64,1024]{3,0,1,2:T(1,128)}, u32[]{:S(2)}, u32[]{:S(2)}) async-start(f32[1,5,64,1024]{3,0,1,2:T(1,128)} %copy.28), calls=%async_computation.1 | async-start | bytes 2621440 | tf_op jit(solution)/shard_map/all_to_all | solution.py:108
  148.6 1.6 maximum_subtract_fusion.1
  151.5 2.3 %collective-permute-start.1 = (f32[1,5,16]{2,0,1:T(1,128)S(1)}, f32[1,5,16]{2,0,1:T(1,128)S(1)}, u32[]{:S(2)}, u32[]{:S(2)}) collective-permute-start(f32[1,5,16]{2,0,1:T(1,128)S(1)} %collective-permute-done), channel_id=1, source_target_pairs={{0,4},{4,8},{8,12},{12,16},{16,20},{20,24},{24,28},{28,0},{1,5},{5... | collective-permute-start | bytes 968 | tf_op jit(solution)/shard_map/ppermute | solution.py:25
  154.5 3.9 %collective-permute-done.1 = f32[1,5,16]{2,0,1:T(1,128)S(1)} collective-permute-done((f32[1,5,16]{2,0,1:T(1,128)S(1)}, f32[1,5,16]{2,0,1:T(1,128)S(1)}, u32[]{:S(2)}, u32[]{:S(2)}) %collective-permute-start.1) | collective-permute-done | bytes 352 | tf_op jit(solution)/shard_map/ppermute | solution.py:25
  158.5 6.3 %collective-permute-done.2 = f32[1,5,16]{2,0,1:T(1,128)S(1)} collective-permute-done((f32[1,5,16]{2,0,1:T(1,128)S(1)}, f32[1,5,16]{2,0,1:T(1,128)S(1)}, u32[]{:S(2)}, u32[]{:S(2)}) %collective-permute-start.2) | collective-permute-done | bytes 352 | tf_op jit(solution)/shard_map/ppermute | solution.py:25
  164.7 6.3 %collective-permute-done.3 = f32[1,5,16]{2,0,1:T(1,128)S(1)} collective-permute-done((f32[1,5,16]{2,0,1:T(1,128)S(1)}, f32[1,5,16]{2,0,1:T(1,128)S(1)}, u32[]{:S(2)}, u32[]{:S(2)}) %collective-permute-start.3) | collective-permute-done | bytes 352 | tf_op jit(solution)/shard_map/ppermute | solution.py:25
  171.0 6.3 %collective-permute-done.4 = f32[1,5,16]{2,0,1:T(1,128)S(1)} collective-permute-done((f32[1,5,16]{2,0,1:T(1,128)S(1)}, f32[1,5,16]{2,0,1:T(1,128)S(1)}, u32[]{:S(2)}, u32[]{:S(2)}) %collective-permute-start.4) | collective-permute-done | bytes 352 | tf_op jit(solution)/shard_map/ppermute | solution.py:25
  177.3 6.3 %collective-permute-done.5 = f32[1,5,16]{2,0,1:T(1,128)S(1)} collective-permute-done((f32[1,5,16]{2,0,1:T(1,128)S(1)}, f32[1,5,16]{2,0,1:T(1,128)S(1)}, u32[]{:S(2)}, u32[]{:S(2)}) %collective-permute-start.5) | collective-permute-done | bytes 352 | tf_op jit(solution)/shard_map/ppermute | solution.py:25
  183.6 6.3 %collective-permute-done.6 = f32[1,5,16]{2,0,1:T(1,128)S(1)} collective-permute-done((f32[1,5,16]{2,0,1:T(1,128)S(1)}, f32[1,5,16]{2,0,1:T(1,128)S(1)}, u32[]{:S(2)}, u32[]{:S(2)}) %collective-permute-start.6) | collective-permute-done | bytes 352 | tf_op jit(solution)/shard_map/ppermute | solution.py:25
  190.4 1.6 copy.29
  192.0 2.1 %fusion.6 = f32[1,5,16,4096]{3,2,1,0:T(8,128)S(1)} fusion(f32[1,5,16,4096]{3,2,1,0:T(8,128)S(1)} %bitcast.53, f32[1,5,16,4102]{3,2,1,0:T(8,128)S(1)} %maximum_subtract_fusion.1, pred[4096]{0:T(1024)(128)(4,1)S(1)} %get-tuple-element.59, pred[4096]{0:T(1024)(128)(4,1)S(1)} %get-tuple-element.58, pred[4096]{0:T(1024)(128)(4,1)S(1)} %get-tuple-element.56, ...), kind=kLoop, calls=%fused_computation.39 | loop fusion | flops 6225920 | bytes 11812864 | tf_op jit(solution)/shard_map/add | solution.py:111
  194.2 1.0 copy-done
  195.3 1.8 scatter-add.4
  197.1 2.7 %multiply_reduce_fusion = f32[]{:T(128)} fusion(f32[1,5,16,4096]{3,2,1,0:T(8,128)} %param.14, f32[1,5,16,4096]{3,2,1,0:T(8,128)} %scatter-add.4), kind=kLoop, calls=%fused_computation.50 | loop fusion | flops 655359 | bytes 2621444 | tf_op jit(solution)/shard_map/reduce_sum | solution.py:129
  199.7 6.3 %psum.7 = f32[]{:T(128)} all-reduce(f32[]{:T(128)} %multiply_reduce_fusion), channel_id=1, replica_groups=mesh['blk'=8,'line'=4] {'line'}, use_global_device_ids=true, to_apply=%region_5.6 | all-reduce | flops 1 | bytes 8 | tf_op jit(solution)/shard_map/psum | solution.py:129
  (49 shorter events, 6.1 us)
Async XLA Ops:
  60.8 21.5 %all-to-all-start = ((f32[4,1,81920]{2,1,0:T(1,128)}), f32[4,1,81920]{2,1,0:T(1,128)S(1)}, u32[]{:S(2)}, u32[]{:S(2)}) async-start(f32[4,1,81920]{2,1,0:T(1,128)} %reshape.473), calls=%async_computation | async-start | bytes 2621440 | tf_op jit(solution)/shard_map/all_to_all | solution.py:105
  65.1 86.4 %collective-permute-start = (f32[1,5,16]{2,0,1:T(1,128)S(1)}, f32[1,5,16]{2,0,1:T(1,128)S(1)}, u32[]{:S(2)}, u32[]{:S(2)}) collective-permute-start(f32[1,5,16]{2,0,1:T(1,128)S(1)} %squeeze.9), channel_id=1, source_target_pairs={{0,4},{4,8},{8,12},{12,16},{16,20},{20,24},{24,28},{28,0},{1,5},{5... | collective-permute-start | bytes 968 | tf_op jit(solution)/shard_map/ppermute | solution.py:25
  144.3 46.1 %all-to-all-start.1 = ((f32[1,5,64,1024]{3,0,1,2:T(1,128)}), f32[1,5,64,1024]{3,0,1,2:T(1,128)}, u32[]{:S(2)}, u32[]{:S(2)}) async-start(f32[1,5,64,1024]{3,0,1,2:T(1,128)} %copy.28), calls=%async_computation.1 | async-start | bytes 2621440 | tf_op jit(solution)/shard_map/all_to_all | solution.py:108
  148.6 2.3 %copy-start.1 = (s32[1,4]{1,0:T(1,128)S(1)}, s32[1,4]{1,0:T(1,128)}, u32[]{:S(2)}) copy-start(s32[1,4]{1,0:T(1,128)} %param.17) | copy-start | bytes 52
  148.6 41.4 %copy-start.2 = (s32[1,4]{1,0:T(1,128)S(1)}, s32[1,4]{1,0:T(1,128)}, u32[]{:S(2)}) copy-start(s32[1,4]{1,0:T(1,128)} %param.15) | copy-start | bytes 52
  151.5 6.9 %collective-permute-start.1 = (f32[1,5,16]{2,0,1:T(1,128)S(1)}, f32[1,5,16]{2,0,1:T(1,128)S(1)}, u32[]{:S(2)}, u32[]{:S(2)}) collective-permute-start(f32[1,5,16]{2,0,1:T(1,128)S(1)} %collective-permute-done), channel_id=1, source_target_pairs={{0,4},{4,8},{8,12},{12,16},{16,20},{20,24},{24,28},{28,0},{1,5},{5... | collective-permute-start | bytes 968 | tf_op jit(solution)/shard_map/ppermute | solution.py:25
  158.5 6.3 %collective-permute-start.2 = (f32[1,5,16]{2,0,1:T(1,128)S(1)}, f32[1,5,16]{2,0,1:T(1,128)S(1)}, u32[]{:S(2)}, u32[]{:S(2)}) collective-permute-start(f32[1,5,16]{2,0,1:T(1,128)S(1)} %collective-permute-done.1), channel_id=1, source_target_pairs={{0,4},{4,8},{8,12},{12,16},{16,20},{20,24},{24,28},{28,0},{1,5},{5... | collective-permute-start | bytes 968 | tf_op jit(solution)/shard_map/ppermute | solution.py:25
  164.7 6.3 %collective-permute-start.3 = (f32[1,5,16]{2,0,1:T(1,128)S(1)}, f32[1,5,16]{2,0,1:T(1,128)S(1)}, u32[]{:S(2)}, u32[]{:S(2)}) collective-permute-start(f32[1,5,16]{2,0,1:T(1,128)S(1)} %collective-permute-done.2), channel_id=1, source_target_pairs={{0,4},{4,8},{8,12},{12,16},{16,20},{20,24},{24,28},{28,0},{1,5},{5... | collective-permute-start | bytes 968 | tf_op jit(solution)/shard_map/ppermute | solution.py:25
  171.0 6.3 %collective-permute-start.4 = (f32[1,5,16]{2,0,1:T(1,128)S(1)}, f32[1,5,16]{2,0,1:T(1,128)S(1)}, u32[]{:S(2)}, u32[]{:S(2)}) collective-permute-start(f32[1,5,16]{2,0,1:T(1,128)S(1)} %collective-permute-done.3), channel_id=1, source_target_pairs={{0,4},{4,8},{8,12},{12,16},{16,20},{20,24},{24,28},{28,0},{1,5},{5... | collective-permute-start | bytes 968 | tf_op jit(solution)/shard_map/ppermute | solution.py:25
  177.3 6.3 %collective-permute-start.5 = (f32[1,5,16]{2,0,1:T(1,128)S(1)}, f32[1,5,16]{2,0,1:T(1,128)S(1)}, u32[]{:S(2)}, u32[]{:S(2)}) collective-permute-start(f32[1,5,16]{2,0,1:T(1,128)S(1)} %collective-permute-done.4), channel_id=1, source_target_pairs={{0,4},{4,8},{8,12},{12,16},{16,20},{20,24},{24,28},{28,0},{1,5},{5... | collective-permute-start | bytes 968 | tf_op jit(solution)/shard_map/ppermute | solution.py:25
  183.6 6.3 %collective-permute-start.6 = (f32[1,5,16]{2,0,1:T(1,128)S(1)}, f32[1,5,16]{2,0,1:T(1,128)S(1)}, u32[]{:S(2)}, u32[]{:S(2)}) collective-permute-start(f32[1,5,16]{2,0,1:T(1,128)S(1)} %collective-permute-done.5), channel_id=1, source_target_pairs={{0,4},{4,8},{8,12},{12,16},{16,20},{20,24},{24,28},{28,0},{1,5},{5... | collective-permute-start | bytes 968 | tf_op jit(solution)/shard_map/ppermute | solution.py:25
  194.1 1.1 copy-start
